TPU v7x, 32 devices: a whole 2x2x4 slice. The times are simulated.
32 devices in a mesh: section: 2 (over core), egroup: 4 (over y, x), fsdp: 4 (over z).
Axes of the slice: x: 2, y: 2, z: 4, core: 2. Of those that a mesh axis runs over, the one named last changes fastest.
Arguments:
- tokens: bfloat16 [4096, 2048], P(('section', 'egroup', 'fsdp')), may hold values from -6 to 6
- expert_ids: int32 [4096, 2], P(('section', 'egroup', 'fsdp')), may hold values from 0 to 3, all different within a row; in each aligned block of 128 rows (0 to 127, 128 to 255, ...) at most 96 rows name the same one
- gate_weights: float32 [4096, 2], P(('section', 'egroup', 'fsdp')), may hold values from 0.25 to 1
- w_in: bfloat16 [4, 2048, 4096], P('egroup', 'fsdp', 'section'), may hold values from -0.125 to 0.125
- w_out: bfloat16 [4, 4096, 2048], P('egroup', 'section', 'fsdp'), may hold values from -0.09375 to 0.09375
Outputs:
- mixed: bfloat16 [4096, 2048], P(('section', 'egroup', 'fsdp'))
Inputs may be any that keep to these rules, and one draw needn't show every extreme that they name: `expert_ids`: the two experts of a token differ. Among the 128 tokens of one device (aligned blocks of rows), at most 96 name any one expert, a bound that some block reaches.
All inputs are finite; a program needn't handle non-finite values.
Results may differ from a plain program's by a relative error of at most 0.0065.
Values may be sent and summed in bfloat16 or wider, within the bound.
A program may use at most 128 MiB of HBM per device.

v0:
```python
import jax
import jax.numpy as jnp
from jax import lax
from jax.sharding import PartitionSpec as P


def per_device(tokens, expert_ids, gate_weights, w_in, w_out):
    group_count = lax.axis_size("egroup")
    tok_rows = tokens.shape[0]
    slot_cap = 3 * tok_rows // group_count
    width = tokens.shape[1]
    block_rows = 128
    flat_ids = expert_ids.reshape(-1)
    one_hot = (flat_ids[:, None] == jnp.arange(group_count, dtype=jnp.int32)[None, :]).astype(
        jnp.int32
    )
    earlier = jnp.cumsum(one_hot, axis=0) - one_hot
    position = jnp.sum(earlier * one_hot, axis=1)
    per_expert = jnp.sum(one_hot, axis=0)
    slot_of = (flat_ids * slot_cap + position).reshape(tok_rows, 2)
    slot_range = jnp.arange(group_count * slot_cap, dtype=jnp.int32)
    dispatch_map = jnp.any(slot_of[None, :, :] == slot_range[:, None, None], axis=2).astype(
        jnp.bfloat16
    )
    outgoing = jnp.dot(dispatch_map, tokens, preferred_element_type=jnp.float32).astype(
        jnp.bfloat16
    )
    outgoing = outgoing.reshape(group_count, slot_cap, width)
    arrived, arrived_counts = (
        lax.all_to_all(outgoing, "egroup", split_axis=0, concat_axis=0, tiled=True),
        lax.all_to_all(
            per_expert.reshape(group_count, 1), "egroup", split_axis=0, concat_axis=0, tiled=True
        ),
    )
    paired, paired_counts = (
        lax.all_gather(arrived, "section", axis=0, tiled=True),
        lax.all_gather(arrived_counts, "section", axis=0, tiled=True),
    )
    sources = paired.shape[0]
    total_rows = sources * slot_cap
    source_counts = paired_counts[:, 0]
    source_ends = jnp.cumsum(source_counts)
    source_starts = source_ends - source_counts
    live_total = source_ends[-1]
    packed_pos = jnp.arange(total_rows, dtype=jnp.int32)
    source_of = jnp.minimum(
        jnp.sum((source_ends[None, :] <= packed_pos[:, None]).astype(jnp.int32), axis=1),
        sources - 1,
    )
    within = packed_pos - source_starts[source_of]
    is_live = packed_pos < live_total
    gather_index = jnp.where(is_live, source_of * slot_cap + within, 0)
    flat_rows = paired.reshape(total_rows, width)
    packed = jnp.where(
        is_live[:, None], flat_rows[gather_index], jnp.zeros_like(flat_rows[gather_index])
    )
    block_count = (live_total + block_rows - 1) // block_rows
    first_local = w_in[0]
    second_local = w_out[0]
    first_full, second_full = (
        lax.all_gather(first_local, "fsdp", axis=0, tiled=True),
        lax.all_gather(second_local, "fsdp", axis=1, tiled=True),
    )

    def whole_block(block, totals):
        first_row = block * block_rows
        block_in = lax.dynamic_slice_in_dim(packed, first_row, block_rows, 0)
        hidden = jnp.dot(block_in, first_full, preferred_element_type=jnp.float32)
        activated = jax.nn.gelu(hidden, approximate=False).astype(jnp.bfloat16)
        result = jnp.dot(activated, second_full, preferred_element_type=jnp.float32)
        return lax.dynamic_update_slice_in_dim(totals, result, first_row, 0)

    partial_out = lax.fori_loop(
        0, block_count, whole_block, jnp.zeros((total_rows, width), jnp.float32)
    )
    slot_source = jnp.arange(total_rows, dtype=jnp.int32) // slot_cap
    slot_within = jnp.arange(total_rows, dtype=jnp.int32) % slot_cap
    slot_valid = slot_within < source_counts[slot_source]
    slot_target = jnp.where(slot_valid, source_starts[slot_source] + slot_within, 0)
    slot_values = jnp.where(
        slot_valid[:, None], partial_out[slot_target], jnp.zeros_like(partial_out[slot_target])
    )
    slot_values = slot_values.reshape(2, group_count, slot_cap, width)
    summed = lax.psum_scatter(
        slot_values.astype(jnp.bfloat16), "section", scatter_dimension=0, tiled=True
    ).astype(jnp.float32)
    finished = summed.reshape(group_count, slot_cap, width).astype(jnp.bfloat16)
    came_back = lax.all_to_all(finished, "egroup", split_axis=0, concat_axis=0, tiled=True)
    back_rows = came_back.reshape(group_count * slot_cap, width)
    picked = back_rows[slot_of.reshape(-1)].reshape(tok_rows, 2, width).astype(jnp.float32)
    return jnp.sum(gate_weights[:, :, None] * picked, axis=1).astype(jnp.bfloat16)


def solution(mesh):
    placed = (
        P(("section", "egroup", "fsdp"), None),
        P(("section", "egroup", "fsdp"), None),
        P(("section", "egroup", "fsdp"), None),
        P("egroup", "fsdp", "section"),
        P("egroup", "section", "fsdp"),
    )
    return jax.shard_map(
        per_device,
        mesh=mesh,
        in_specs=placed,
        out_specs=P(("section", "egroup", "fsdp"), None),
        check_vma=False,
    )
```

profile of v0, /device:TPU:0, one launch (start us, length us, event | category | flops | bytes accessed | tf_op | source)
XLA Modules:
  0.0 479.3 jit_solution(10715246494147592483)
XLA Ops:
  10.3 24.8 %all_to_all.22 = bf16[4,96,2048]{2,1,0:T(8,128)(2,1)} all-to-all(bf16[4,96,2048]{2,1,0:T(8,128)(2,1)S(1)} %bitcast.53), channel_id=1, replica_groups=mesh['section'=2,'egroup'=4,'fsdp'=4] {'egroup'}, dimensions={0} | all-to-all | bytes 3145728 | tf_op jit(solution)/shard_map/all_to_all | solution.py:30
  37.3 3.2 all-to-all-start
  41.9 3.1 all-to-all-done
  49.5 4.5 fusion.84
  54.7 4.5 fusion.83
  62.5 9.6 %gather_fusion = bf16[768,2048]{1,0:T(8,128)(2,1)} fusion(bf16[768,2048]{1,0:T(8,128)(2,1)} %bitcast.50, s32[1024]{0:T(1024)S(1)} %pad_clamp_fusion.2), kind=kCustom, calls=%fused_computation | custom fusion | bytes 6294528 | tf_op jit(solution)/shard_map/gather | solution.py:55
  72.1 3.9 broadcast_select_fusion
  75.9 123.6 %all-gather.9.cloned.1.call-done = bf16[1,2048,2048]{2,1,0:T(8,128)(2,1)} async-done(((bf16[1,512,2048]{2,1,0:T(8,128)(2,1)}), bf16[1,2048,2048]{2,1,0:T(8,128)(2,1)}) %all-gather.9.cloned.1.call-update) | async-done | bytes 8388624 | tf_op jit(solution)/shard_map/all_gather | solution.py:61
  199.6 149.5 %all-gather.11.cloned.1.call-done = bf16[1,2048,2048]{2,1,0:T(8,128)(2,1)} async-done(((bf16[1,2048,512]{2,1,0:T(8,128)(2,1)}), bf16[1,2048,2048]{2,1,0:T(8,128)(2,1)}) %all-gather.11.cloned.1.call-update) | async-done | bytes 8388624 | tf_op jit(solution)/shard_map/all_gather | solution.py:62
  351.1 68.8 %while.10 = (s32[]{:T(128)}, bf16[768,2048]{1,0:T(8,128)(2,1)}, s32[]{:T(128)}, bf16[768,2048]{1,0:T(8,128)(2,1)}, bf16[2048,2048]{1,0:T(8,128)(2,1)}, /*index=5...) while((s32[]{:T(128)}, bf16[768,2048]{1,0:T(8,128)(2,1)}, s32[]{:T(128)}, ...), condition=%wide.region_8.9_spmd, body=%wide.region_7.8_spmd.sunk | while | flops 2164523008 | bytes 18351252 | solution.py:73
  351.1 11.4 %convolution_dynamic-update-slice_fusion.2 = bf16[768,2048]{1,0:T(8,128)(2,1)} fusion(bf16[768,2048]{1,0:T(8,128)(2,1)} %get-tuple-element.124, s32[]{:T(128)S(6)} %select_n.182, bf16[2048,2048]{1,0:T(8,128)(2,1)} %get-tuple-element.138, bf16[2048,2048]{1,0:T(8,128)(2,1)} %get-tuple-element.137, bf16[768,2048]{1,0:T(8,128)(2,1)} %get-tuple-element.136), kind=kOutput, calls=%fused_computation.3.clone.1 | convolution fusion | flops 2164523008 | bytes 18351104 | tf_op jit(solution)/shard_map/while/body/dot_general | solution.py:70
  362.5 11.5 %convolution_dynamic-update-slice_fusion.2 = bf16[768,2048]{1,0:T(8,128)(2,1)} fusion(bf16[768,2048]{1,0:T(8,128)(2,1)} %get-tuple-element.124, s32[]{:T(128)S(6)} %select_n.182, bf16[2048,2048]{1,0:T(8,128)(2,1)} %get-tuple-element.138, bf16[2048,2048]{1,0:T(8,128)(2,1)} %get-tuple-element.137, bf16[768,2048]{1,0:T(8,128)(2,1)} %get-tuple-element.136), kind=kOutput, calls=%fused_computation.3.clone.1 | convolution fusion | flops 2164523008 | bytes 18351104 | tf_op jit(solution)/shard_map/while/body/dot_general | solution.py:70
  374.0 11.5 %convolution_dynamic-update-slice_fusion.2 = bf16[768,2048]{1,0:T(8,128)(2,1)} fusion(bf16[768,2048]{1,0:T(8,128)(2,1)} %get-tuple-element.124, s32[]{:T(128)S(6)} %select_n.182, bf16[2048,2048]{1,0:T(8,128)(2,1)} %get-tuple-element.138, bf16[2048,2048]{1,0:T(8,128)(2,1)} %get-tuple-element.137, bf16[768,2048]{1,0:T(8,128)(2,1)} %get-tuple-element.136), kind=kOutput, calls=%fused_computation.3.clone.1 | convolution fusion | flops 2164523008 | bytes 18351104 | tf_op jit(solution)/shard_map/while/body/dot_general | solution.py:70
  385.5 11.5 %convolution_dynamic-update-slice_fusion.2 = bf16[768,2048]{1,0:T(8,128)(2,1)} fusion(bf16[768,2048]{1,0:T(8,128)(2,1)} %get-tuple-element.124, s32[]{:T(128)S(6)} %select_n.182, bf16[2048,2048]{1,0:T(8,128)(2,1)} %get-tuple-element.138, bf16[2048,2048]{1,0:T(8,128)(2,1)} %get-tuple-element.137, bf16[768,2048]{1,0:T(8,128)(2,1)} %get-tuple-element.136), kind=kOutput, calls=%fused_computation.3.clone.1 | convolution fusion | flops 2164523008 | bytes 18351104 | tf_op jit(solution)/shard_map/while/body/dot_general | solution.py:70
  397.0 11.4 %convolution_dynamic-update-slice_fusion.2 = bf16[768,2048]{1,0:T(8,128)(2,1)} fusion(bf16[768,2048]{1,0:T(8,128)(2,1)} %get-tuple-element.124, s32[]{:T(128)S(6)} %select_n.182, bf16[2048,2048]{1,0:T(8,128)(2,1)} %get-tuple-element.138, bf16[2048,2048]{1,0:T(8,128)(2,1)} %get-tuple-element.137, bf16[768,2048]{1,0:T(8,128)(2,1)} %get-tuple-element.136), kind=kOutput, calls=%fused_computation.3.clone.1 | convolution fusion | flops 2164523008 | bytes 18351104 | tf_op jit(solution)/shard_map/while/body/dot_general | solution.py:70
  408.4 11.5 %convolution_dynamic-update-slice_fusion.2 = bf16[768,2048]{1,0:T(8,128)(2,1)} fusion(bf16[768,2048]{1,0:T(8,128)(2,1)} %get-tuple-element.124, s32[]{:T(128)S(6)} %select_n.182, bf16[2048,2048]{1,0:T(8,128)(2,1)} %get-tuple-element.138, bf16[2048,2048]{1,0:T(8,128)(2,1)} %get-tuple-element.137, bf16[768,2048]{1,0:T(8,128)(2,1)} %get-tuple-element.136), kind=kOutput, calls=%fused_computation.3.clone.1 | convolution fusion | flops 2164523008 | bytes 18351104 | tf_op jit(solution)/shard_map/while/body/dot_general | solution.py:70
  419.9 9.4 %gather_fusion.1 = bf16[768,2048]{1,0:T(8,128)(2,1)} fusion(bf16[768,2048]{1,0:T(8,128)(2,1)} %get-tuple-element.38, s32[1024]{0:T(1024)S(1)} %pad_clamp_fusion.1), kind=kCustom, calls=%fused_computation.1 | custom fusion | bytes 6294528 | tf_op jit(solution)/shard_map/gather | solution.py:81
  429.3 4.2 select_convert_fusion
  433.5 6.9 %reduce-scatter.2.cloned.1.call-done = bf16[1,4,96,2048]{3,2,1,0:T(8,128)(2,1)} async-done(((bf16[2,4,96,2048]{3,2,1,0:T(8,128)(2,1)}), bf16[1,4,96,2048]{3,2,1,0:T(8,128)(2,1)}) %reduce-scatter.2.cloned.1.call-update) | async-done | bytes 1572880 | tf_op jit(solution)/shard_map/reduce_scatter | solution.py:84
  440.5 3.9 all-to-all-start.2
  444.6 19.4 %all-to-all-done.2 = bf16[4,96,2048]{2,1,0:T(8,128)(2,1)S(1)} async-done(((bf16[4,96,2048]{2,1,0:T(8,128)(2,1)}), bf16[4,96,2048]{2,1,0:T(8,128)(2,1)S(1)}, u32[]{:S(2)}, u32[]{:S(2)}) %all-to-all-start.2) | async-done | bytes 1572896 | tf_op jit(solution)/shard_map/all_to_all | solution.py:88
  464.1 2.3 gather_fusion.2
  466.4 2.4 reshape.235
  468.8 3.9 multiply_reduce_fusion
  (61 shorter events, 16.5 us)
Async XLA Ops:
  6.5 3.2 copy-start
  6.5 55.9 %all-gather.7.cloned.1.call-start = ((), (), s32[]{:S(2)}) async-start(), calls=%async_computation.4 | async-start | bytes 4718592 | tf_op jit(solution)/shard_map/all_gather | solution.py:36
  35.1 5.5 %copy-start.2 = (u32[32]{0:T(128)S(1)}, u32[32]{0:T(128)}, u32[]{:S(2)}) copy-start(u32[32]{0:T(128)} %constant.160) | copy-start | bytes 388
  35.1 164.4 %all-gather.9.cloned.1.call-start = ((), (), s32[]{:S(2)}) async-start(), calls=%async_computation.6 | async-start | bytes 10485760 | tf_op jit(solution)/shard_map/all_gather | solution.py:61
  35.9 313.1 %all-gather.11.cloned.1.call-start = ((), (), s32[]{:S(2)}) async-start(), calls=%async_computation.7 | async-start | bytes 10485760 | tf_op jit(solution)/shard_map/all_gather | solution.py:62
  37.3 7.8 %all-to-all-start = ((s32[4,1,1]{2,1,0:T(1,128)}), s32[4,1,1]{2,1,0:T(1,128)S(1)}, u32[]{:S(2)}, u32[]{:S(2)}) async-start(s32[4,1,1]{2,1,0:T(1,128)} %copy.32), calls=%async_computation | async-start | bytes 4096 | tf_op jit(solution)/shard_map/all_to_all | solution.py:31
  40.5 399.9 %reduce-scatter.2.cloned.1.call-start = ((), (), s32[]{:S(2)}) async-start(), calls=%async_computation.5 | async-start | bytes 4718592 | tf_op jit(solution)/shard_map/reduce_scatter | solution.py:84
  433.5 11.0 %copy-start.1 = (f32[128,2]{0,1:T(2,128)S(1)}, f32[128,2]{0,1:T(2,128)}, u32[]{:S(2)}) copy-start(f32[128,2]{0,1:T(2,128)} %param.9) | copy-start | bytes 3076
  440.5 23.6 %all-to-all-start.2 = ((bf16[4,96,2048]{2,1,0:T(8,128)(2,1)}), bf16[4,96,2048]{2,1,0:T(8,128)(2,1)S(1)}, u32[]{:S(2)}, u32[]{:S(2)}) async-start(bf16[4,96,2048]{2,1,0:T(8,128)(2,1)} %bitcast.54), calls=%async_computation.3 | async-start | bytes 3145728 | tf_op jit(solution)/shard_map/all_to_all | solution.py:88
Sparse Core Ops, SparseCore 0:
  35.3 11.8 all-gather.6
  48.7 150.8 all-gather.8
  201.2 147.8 all-gather.10
  433.7 6.7 reduce-scatter.1
where the time goes:
time: 480 us; the launch traced here: 479 us
  waiting for transfers between devices  304 us (63%)
  matrix products  69.4 us (14%)
  local copies, waits for them, and re-layouts  31.3 us (7%)
  blocking collectives  26.6 us (6%)
  other arithmetic  26.1 us (5%)
  between operations  14.6 us (3%)
  starting transfers between devices  7.22 us (2%)
    all_gather x1, waiting for transfers between devices, per_device(): lax.all_gather(second_local, 'fsdp', axis=1, tiled=True)  149 us
    all_gather x1, waiting for transfers between devices, per_device(): lax.all_gather(first_local, 'fsdp', axis=0, tiled=True)  124 us
    dot_general x6, matrix products, whole_block(): result = jnp.dot(activated, second_full, preferred_element_type=jnp.float32)  68.8 us
    all_to_all x1, blocking collectives, per_device(): lax.all_to_all(outgoing, 'egroup', split_axis=0, concat_axis=0, tiled=True)  24.8 us
    all_to_all x1, waiting for transfers between devices, per_device(): lax.all_to_all(finished, 'egroup', split_axis=0, concat_axis=0, tiled=True)  19.4 us
    gather x1, local copies, waits for them, and re-layouts, per_device(): flat_rows[gather_index]  9.6 us
  transfers between devices with their start and end apart: 6, of which 5 were waited for; matrix products, arithmetic and copies ran while one was open for 6% of the time, Pallas kernels for 0%

commit v1 on v0

v1 whole, which is shorter than its diff:
```python
import jax
import jax.numpy as jnp
from jax import lax
from jax.sharding import PartitionSpec as P

EVERY = ("section", "egroup", "fsdp")


def per_device(tokens, expert_ids, gate_weights, w_in, w_out):
    rows, width = tokens.shape
    devices = lax.axis_size("section") * lax.axis_size("egroup") * lax.axis_size("fsdp")
    chunks = 4
    step = rows // chunks
    mine = lax.axis_index("egroup")
    first = lax.all_to_all(w_in[0], "fsdp", split_axis=1, concat_axis=0, tiled=True)
    second = lax.all_to_all(w_out[0], "fsdp", split_axis=0, concat_axis=1, tiled=True)
    ids = lax.all_gather(expert_ids, EVERY, axis=0)
    gates = lax.all_gather(gate_weights, EVERY, axis=0)
    weight = jnp.sum(jnp.where(ids == mine, gates, 0.0), axis=2)
    outs = []
    for chunk in range(chunks):
        part = tokens[chunk * step:(chunk + 1) * step]
        part = lax.all_gather(part, "fsdp", axis=0, tiled=True)
        part = lax.all_gather(part, ("section", "egroup"), axis=0, tiled=True)
        hidden = jnp.dot(part, first, preferred_element_type=jnp.float32)
        activated = jax.nn.gelu(hidden, approximate=False).astype(jnp.bfloat16)
        result = jnp.dot(activated, second, preferred_element_type=jnp.float32)
        scale = weight[:, chunk * step:(chunk + 1) * step].reshape(devices * step, 1)
        result = (result * scale).astype(jnp.bfloat16)
        result = lax.psum_scatter(result, ("section", "egroup"), scatter_dimension=0, tiled=True)
        result = lax.psum_scatter(result, "fsdp", scatter_dimension=0, tiled=True)
        outs.append(result)
    return jnp.concatenate(outs, axis=0)


def solution(mesh):
    placed = (
        P(EVERY, None),
        P(EVERY, None),
        P(EVERY, None),
        P("egroup", "fsdp", "section"),
        P("egroup", "section", "fsdp"),
    )
    return jax.shard_map(
        per_device,
        mesh=mesh,
        in_specs=placed,
        out_specs=P(EVERY, None),
        check_vma=False,
    )
```

time: 480 us -> 634 us (1.32)
  blocking collectives: 26.6 us -> 270 us
  waiting for transfers between devices: 304 us -> 278 us
  other arithmetic: 26.1 us -> 1.98 us
  local copies, waits for them, and re-layouts: 31.3 us -> 10.9 us
  matrix products: 69.4 us -> 50.4 us
    all_gather x3 -> x4, waiting for transfers between devices: 273 us -> 0.01 us  [per_device(): part = lax.all_gather(part, ('section', 'egroup'), axis=0, tiled=True)]
    reduce_scatter x1 -> x8, waiting for transfers between devices: 6.94 us -> 277 us  [the longest x4 187 us: per_device(): lax.psum_scatter(result, ('section', 'egroup'), scatter_dimension=0, tile...]
    all_gather x0 -> x6, blocking collectives: none -> 270 us  [the longest x4 105 us: per_device(): part = lax.all_gather(part, 'fsdp', axis=0, tiled=True)]
    all_to_all x1 -> x0, blocking collectives: 24.8 us -> none  [per_device(): lax.all_to_all(outgoing, 'egroup', split_axis=0, concat_axis=0, tiled=True)]
    gather x6 -> x0, local copies, waits for them, and re-layouts: 22.8 us -> none  [the longest x1 9.6 us: per_device(): flat_rows[gather_index]]
    all_to_all x2, waiting for transfers between devices: 22.6 us -> 0.01 us  [the longest x1 0.01 us: per_device(): lax.all_to_all(w_out[0], 'fsdp', split_axis=0, concat_axis=1, tiled=True)]
    dot_general x7 -> x4, matrix products: 69.4 us -> 50.4 us  [per_device(): result = jnp.dot(activated, second, preferred_element_type=jnp.float32)]
    gather x9 -> x0, other arithmetic: 10.8 us -> none  [the longest x3 5.6 us: per_device(): slot_valid = slot_within < source_counts[slot_source]]
  transfers between devices with their start and end apart: 6 -> 14, of which waited for: 5 -> 8; matrix products, arithmetic and copies ran while one was open for 6% -> 9% of each run, Pallas kernels for 0% -> 0%
where the time goes in v1:
time: 634 us
  waiting for transfers between devices  278 us (44%)
  blocking collectives  270 us (43%)
  matrix products  50.4 us (8%)
  between operations  13.6 us (2%)
  local copies, waits for them, and re-layouts  10.9 us (2%)
  starting transfers between devices  8.93 us (1%)
    reduce_scatter x4, waiting for transfers between devices, per_device(): lax.psum_scatter(result, ('section', 'egroup'), scatter_dimension=0, tile...  187 us
    all_gather x4, blocking collectives, per_device(): part = lax.all_gather(part, 'fsdp', axis=0, tiled=True)  105 us
    all_gather x1, blocking collectives, per_device(): ids = lax.all_gather(expert_ids, EVERY, axis=0)  99.8 us
    reduce_scatter x4, waiting for transfers between devices, per_device(): result = lax.psum_scatter(result, 'fsdp', scatter_dimension=0, tiled=True)  90.2 us
    all_gather x1, blocking collectives, per_device(): gates = lax.all_gather(gate_weights, EVERY, axis=0)  65.5 us
    dot_general x4, matrix products, per_device(): result = jnp.dot(activated, second, preferred_element_type=jnp.float32)  50.4 us
  transfers between devices with their start and end apart: 14, of which 8 were waited for; matrix products, arithmetic and copies ran while one was open for 9% of the time, Pallas kernels for 0%

profile of v1, /device:TPU:0, one launch (start us, length us, event | category | flops | bytes accessed | tf_op | source)
XLA Modules:
  0.0 634.0 jit_solution(15587576410114348586)
XLA Ops:
  7.8 18.0 %all_gather.36 = bf16[128,2048]{1,0:T(8,128)(2,1)} all-gather(bf16[32,2048]{1,0:T(8,128)(2,1)S(1)} %get-tuple-element.5), channel_id=1, replica_groups=mesh['section'=2,'egroup'=4,'fsdp'=4] {'fsdp'}, dimensions={0}, use_global_device_ids=true | all-gather | bytes 655360 | tf_op jit(solution)/shard_map/all_gather | solution.py:23
  25.9 17.7 %all_gather.42 = bf16[128,2048]{1,0:T(8,128)(2,1)} all-gather(bf16[32,2048]{1,0:T(8,128)(2,1)S(1)} %get-tuple-element.6), channel_id=1, replica_groups=mesh['section'=2,'egroup'=4,'fsdp'=4] {'fsdp'}, dimensions={0}, use_global_device_ids=true | all-gather | bytes 655360 | tf_op jit(solution)/shard_map/all_gather | solution.py:23
  43.7 16.5 %all_gather.44 = bf16[128,2048]{1,0:T(8,128)(2,1)} all-gather(bf16[32,2048]{1,0:T(8,128)(2,1)S(1)} %get-tuple-element.8), channel_id=1, replica_groups=mesh['section'=2,'egroup'=4,'fsdp'=4] {'fsdp'}, dimensions={0}, use_global_device_ids=true | all-gather | bytes 655360 | tf_op jit(solution)/shard_map/all_gather | solution.py:23
  60.2 2.5 copy.6
  62.7 3.9 all-to-all-start
  66.6 53.0 %all_gather.46 = bf16[128,2048]{1,0:T(8,128)(2,1)} all-gather(bf16[32,2048]{1,0:T(8,128)(2,1)S(1)} %get-tuple-element.7), channel_id=1, replica_groups=mesh['section'=2,'egroup'=4,'fsdp'=4] {'fsdp'}, dimensions={0}, use_global_device_ids=true | all-gather | bytes 655360 | tf_op jit(solution)/shard_map/all_gather | solution.py:23
  119.6 4.5 all-to-all-start.1
  124.2 99.8 %all-gather = s32[4096,2]{0,1:T(2,128)S(1)} all-gather(s32[128,2]{0,1:T(2,128)S(1)} %copy-done.2), channel_id=2, replica_groups=mesh['section'=2,'egroup'=4,'fsdp'=4] {'section','egroup','fsdp'}, dimensions={0}, use_global_device_ids=true | all-gather | bytes 33792 | tf_op jit(solution)/shard_map/all_gather | solution.py:17
  224.0 65.5 %all-gather.1 = f32[4096,2]{0,1:T(2,128)S(1)} all-gather(f32[128,2]{0,1:T(2,128)S(1)} %copy-done.3), channel_id=3, replica_groups=mesh['section'=2,'egroup'=4,'fsdp'=4] {'section','egroup','fsdp'}, dimensions={0}, use_global_device_ids=true | all-gather | bytes 33792 | tf_op jit(solution)/shard_map/all_gather | solution.py:18
  289.7 2.4 copy.7
  292.1 4.3 copy.8
  296.4 12.6 %multiply_convert_fusion.3 = bf16[1024,2048]{1,0:T(8,128)(2,1)} fusion(bf16[512,2048]{0,1:T(8,128)(2,1)} %bitcast.26, f32[1024]{0:T(1024)S(1)} %mul.79, bf16[1024,2048]{1,0:T(8,128)(2,1)} %all-gather.7.cloned.1.call-done, bf16[2048,512]{1,0:T(8,128)(2,1)S(1)} %bitcast.22), kind=kOutput, calls=%fused_computation.3 | convolution fusion | flops 4333240320 | bytes 12587008 | tf_op jit(solution)/shard_map/dot_general | solution.py:27
  309.1 12.6 %multiply_convert_fusion.2 = bf16[1024,2048]{1,0:T(8,128)(2,1)} fusion(bf16[512,2048]{0,1:T(8,128)(2,1)} %bitcast.27, f32[1024]{0:T(1024)S(1)} %mul.85, bf16[1024,2048]{1,0:T(8,128)(2,1)} %all-gather.9.cloned.1.call-done, bf16[2048,512]{1,0:T(8,128)(2,1)S(1)} %bitcast.23), kind=kOutput, calls=%fused_computation.2 | convolution fusion | flops 4333240320 | bytes 12587008 | tf_op jit(solution)/shard_map/dot_general | solution.py:27
  322.0 12.6 %multiply_convert_fusion.1 = bf16[1024,2048]{1,0:T(8,128)(2,1)} fusion(bf16[512,2048]{0,1:T(8,128)(2,1)} %bitcast.28, f32[1024]{0:T(1024)S(1)} %mul.91, bf16[1024,2048]{1,0:T(8,128)(2,1)} %all-gather.11.cloned.1.call-done, bf16[2048,512]{1,0:T(8,128)(2,1)S(1)} %bitcast.24), kind=kOutput, calls=%fused_computation.1 | convolution fusion | flops 4333240320 | bytes 12587008 | tf_op jit(solution)/shard_map/dot_general | solution.py:27
  334.8 12.6 %multiply_convert_fusion = bf16[1024,2048]{1,0:T(8,128)(2,1)} fusion(bf16[512,2048]{0,1:T(8,128)(2,1)} %bitcast.29, f32[1024]{0:T(1024)S(1)} %mul.97, bf16[1024,2048]{1,0:T(8,128)(2,1)} %all-gather.13.cloned.1.call-done, bf16[2048,512]{1,0:T(8,128)(2,1)S(1)} %bitcast.25), kind=kOutput, calls=%fused_computation | convolution fusion | flops 4333240320 | bytes 12587008 | tf_op jit(solution)/shard_map/dot_general | solution.py:27
  347.5 22.7 %reduce-scatter.9.cloned.1.call-done = bf16[128,2048]{1,0:T(8,128)(2,1)} async-done(((bf16[1024,2048]{1,0:T(8,128)(2,1)}), bf16[128,2048]{1,0:T(8,128)(2,1)}) %reduce-scatter.9.cloned.1.call-update) | async-done | bytes 524304 | tf_op jit(solution)/shard_map/reduce_scatter | solution.py:30
  370.3 54.9 %reduce-scatter.13.cloned.1.call-done = bf16[128,2048]{1,0:T(8,128)(2,1)} async-done(((bf16[1024,2048]{1,0:T(8,128)(2,1)}), bf16[128,2048]{1,0:T(8,128)(2,1)}) %reduce-scatter.13.cloned.1.call-update) | async-done | bytes 524304 | tf_op jit(solution)/shard_map/reduce_scatter | solution.py:30
  425.2 54.6 %reduce-scatter.17.cloned.1.call-done = bf16[128,2048]{1,0:T(8,128)(2,1)} async-done(((bf16[1024,2048]{1,0:T(8,128)(2,1)}), bf16[128,2048]{1,0:T(8,128)(2,1)}) %reduce-scatter.17.cloned.1.call-update) | async-done | bytes 524304 | tf_op jit(solution)/shard_map/reduce_scatter | solution.py:30
  479.9 55.0 %reduce-scatter.21.cloned.1.call-done = bf16[128,2048]{1,0:T(8,128)(2,1)} async-done(((bf16[1024,2048]{1,0:T(8,128)(2,1)}), bf16[128,2048]{1,0:T(8,128)(2,1)}) %reduce-scatter.21.cloned.1.call-update) | async-done | bytes 524304 | tf_op jit(solution)/shard_map/reduce_scatter | solution.py:30
  535.0 23.9 %reduce-scatter.11.cloned.1.call-done = bf16[32,2048]{1,0:T(8,128)(2,1)} async-done(((bf16[128,2048]{1,0:T(8,128)(2,1)}), bf16[32,2048]{1,0:T(8,128)(2,1)}) %reduce-scatter.11.cloned.1.call-update) | async-done | bytes 131088 | tf_op jit(solution)/shard_map/reduce_scatter | solution.py:31
  558.9 22.0 %reduce-scatter.15.cloned.1.call-done = bf16[32,2048]{1,0:T(8,128)(2,1)} async-done(((bf16[128,2048]{1,0:T(8,128)(2,1)}), bf16[32,2048]{1,0:T(8,128)(2,1)}) %reduce-scatter.15.cloned.1.call-update) | async-done | bytes 131088 | tf_op jit(solution)/shard_map/reduce_scatter | solution.py:31
  580.9 22.2 %reduce-scatter.19.cloned.1.call-done = bf16[32,2048]{1,0:T(8,128)(2,1)} async-done(((bf16[128,2048]{1,0:T(8,128)(2,1)}), bf16[32,2048]{1,0:T(8,128)(2,1)}) %reduce-scatter.19.cloned.1.call-update) | async-done | bytes 131088 | tf_op jit(solution)/shard_map/reduce_scatter | solution.py:31
  603.1 22.1 %reduce-scatter.23.cloned.1.call-done = bf16[32,2048]{1,0:T(8,128)(2,1)} async-done(((bf16[128,2048]{1,0:T(8,128)(2,1)}), bf16[32,2048]{1,0:T(8,128)(2,1)}) %reduce-scatter.23.cloned.1.call-update) | async-done | bytes 131088 | tf_op jit(solution)/shard_map/reduce_scatter | solution.py:31
  625.2 1.9 pad_maximum_fusion
  (45 shorter events, 2.5 us)
Async XLA Ops:
  6.5 53.6 %copy-start = (bf16[1,512,2048]{2,1,0:T(8,128)(2,1)S(1)}, bf16[1,512,2048]{2,1,0:T(8,128)(2,1)}, u32[]{:S(2)}) copy-start(bf16[1,512,2048]{2,1,0:T(8,128)(2,1)} %param.8) | copy-start | bytes 6291460
  6.5 289.8 %all-gather.7.cloned.1.call-start = ((), (), s32[]{:S(2)}) async-start(), calls=%async_computation.10 | async-start | bytes 4718592 | tf_op jit(solution)/shard_map/all_gather | solution.py:24
  25.8 283.3 %all-gather.9.cloned.1.call-start = ((), (), s32[]{:S(2)}) async-start(), calls=%async_computation.13 | async-start | bytes 4718592 | tf_op jit(solution)/shard_map/all_gather | solution.py:24
  43.6 278.4 %all-gather.11.cloned.1.call-start = ((), (), s32[]{:S(2)}) async-start(), calls=%async_computation.16 | async-start | bytes 4718592 | tf_op jit(solution)/shard_map/all_gather | solution.py:24
  62.7 56.9 %all-to-all-start = ((bf16[512,4,512]{0,2,1:T(8,128)(2,1)}), bf16[512,4,512]{0,2,1:T(8,128)(2,1)S(1)}, u32[]{:S(2)}, u32[]{:S(2)}) async-start(bf16[512,4,512]{0,2,1:T(8,128)(2,1)} %bitcast.20), calls=%async_computation | async-start | bytes 4194304 | tf_op jit(solution)/shard_map/all_to_all | solution.py:15
  66.6 268.2 %all-gather.13.cloned.1.call-start = ((), (), s32[]{:S(2)}) async-start(), calls=%async_computation.19 | async-start | bytes 4718592 | tf_op jit(solution)/shard_map/all_gather | solution.py:24
  119.6 4.6 copy-start.2
  119.6 104.3 %copy-start.3 = (f32[128,2]{0,1:T(2,128)S(1)}, f32[128,2]{0,1:T(2,128)}, u32[]{:S(2)}) copy-start(f32[128,2]{0,1:T(2,128)} %param.7) | copy-start | bytes 3076
  119.6 172.4 %all-to-all-start.1 = ((bf16[4,512,512]{2,1,0:T(8,128)(2,1)}), bf16[4,512,512]{2,1,0:T(8,128)(2,1)}, u32[]{:S(2)}, u32[]{:S(2)}) async-start(bf16[4,512,512]{2,1,0:T(8,128)(2,1)} %bitcast.21), calls=%async_computation.1 | async-start | bytes 4194304 | tf_op jit(solution)/shard_map/all_to_all | solution.py:16
  124.1 246.1 %reduce-scatter.9.cloned.1.call-start = ((), (), s32[]{:S(2)}) async-start(), calls=%async_computation.11 | async-start | bytes 4718592 | tf_op jit(solution)/shard_map/reduce_scatter | solution.py:30
  292.1 4.3 copy-start.1
  309.0 116.2 %reduce-scatter.13.cloned.1.call-start = ((), (), s32[]{:S(2)}) async-start(), calls=%async_computation.14 | async-start | bytes 4718592 | tf_op jit(solution)/shard_map/reduce_scatter | solution.py:30
  321.7 158.1 %reduce-scatter.17.cloned.1.call-start = ((), (), s32[]{:S(2)}) async-start(), calls=%async_computation.17 | async-start | bytes 4718592 | tf_op jit(solution)/shard_map/reduce_scatter | solution.py:30
  334.7 200.3 %reduce-scatter.21.cloned.1.call-start = ((), (), s32[]{:S(2)}) async-start(), calls=%async_computation.20 | async-start | bytes 4718592 | tf_op jit(solution)/shard_map/reduce_scatter | solution.py:30
  347.5 211.4 %reduce-scatter.11.cloned.1.call-start = ((), (), s32[]{:S(2)}) async-start(), calls=%async_computation.12 | async-start | bytes 655360 | tf_op jit(solution)/shard_map/reduce_scatter | solution.py:31
  370.2 210.7 %reduce-scatter.15.cloned.1.call-start = ((), (), s32[]{:S(2)}) async-start(), calls=%async_computation.15 | async-start | bytes 655360 | tf_op jit(solution)/shard_map/reduce_scatter | solution.py:31
  425.2 178.0 %reduce-scatter.19.cloned.1.call-start = ((), (), s32[]{:S(2)}) async-start(), calls=%async_computation.18 | async-start | bytes 655360 | tf_op jit(solution)/shard_map/reduce_scatter | solution.py:31
  479.9 145.4 %reduce-scatter.23.cloned.1.call-start = ((), (), s32[]{:S(2)}) async-start(), calls=%async_computation.21 | async-start | bytes 655360 | tf_op jit(solution)/shard_map/reduce_scatter | solution.py:31
Sparse Core Ops, SparseCore 0:
  26.0 38.6 all-gather.6
  66.6 36.7 all-gather.8
  105.2 36.7 all-gather.10
  143.7 36.7 all-gather.12
  309.1 61.0 reduce-scatter.8
  373.8 51.3 reduce-scatter.12
  428.5 51.2 reduce-scatter.16
  483.6 51.3 reduce-scatter.20
  537.2 21.6 reduce-scatter.10
  561.0 19.8 reduce-scatter.14
  583.2 19.8 reduce-scatter.18
  605.3 19.9 reduce-scatter.22

commit v2 on v1

--- a/solution.py
+++ b/solution.py
@@ -1,12 +1,250 @@
 import jax
 import jax.numpy as jnp
 from jax import lax
+from jax.experimental import pallas as pl
+from jax.experimental.pallas import tpu as pltpu
 from jax.sharding import PartitionSpec as P
 
 EVERY = ("section", "egroup", "fsdp")
-
-
-def per_device(tokens, expert_ids, gate_weights, w_in, w_out):
+MESH = pl.DeviceIdType.MESH
+
+
+def partner(index, step):
+    low = index % 2
+    high = (index // 2) % 2
+    if step % 2:
+        index = index + 1 - 2 * low
+    if step // 2:
+        index = index + 2 - 4 * high
+    return index
+
+
+def gelu(v):
+    return 0.5 * v * (1.0 + lax.erf(v * 0.7071067811865476))
+
+
+def layer_kernel(
+    tokens, gates, w_in, w_out, out,
+    x, first, second, act, sec, plane, ready, zline, gate_all,
+    tz_s, tz_r, tp_s, tp_r, tc_s, tc_r, g_s, g_r, w1_s, w1_r, w2_s, w2_r,
+    sec_s, sec_r, pl_s, pl_r, z_s, z_r, loc,
+):
+    me_s, me_g, me_f = lax.axis_index("section"), lax.axis_index("egroup"), lax.axis_index("fsdp")
+    rows, width = tokens.shape
+    cols = width // 4
+    core = (1 - me_s, me_g, me_f)
+    on_plane = [(me_s, partner(me_g, b), me_f) for b in range(4)]
+    on_line = [(me_s, me_g, partner(me_f, k)) for k in range(4)]
+    partners = [core] + on_plane[1:] + on_line[1:]
+
+    barrier = pltpu.get_barrier_semaphore()
+    for device in partners:
+        pl.semaphore_signal(barrier, inc=1, device_id=device, device_id_type=MESH)
+    pl.semaphore_wait(barrier, len(partners))
+
+    def remote(src, dst, send, recv, device):
+        return pltpu.make_async_remote_copy(
+            src_ref=src, dst_ref=dst, send_sem=send, recv_sem=recv, device_id=device, device_id_type=MESH
+        )
+
+    def block(a, b, k):
+        return x.at[a * 4 + b, pl.ds(k * rows, rows), :]
+
+    def piece(weight, p):
+        return pl.ds(pl.multiple_of(p * (weight // 4), 128), weight // 4)
+
+    hid = w_in.shape[2]
+    token_line = [None] + [
+        remote(tokens, block(0, 0, k), tz_s.at[k], tz_r.at[k], on_line[k]) for k in range(1, 4)
+    ]
+    token_plane = {
+        (b, k): remote(
+            tokens if k == 0 else block(0, 0, k), block(0, b, k), tp_s.at[b, k], tp_r.at[b, k], on_plane[b]
+        )
+        for b in range(1, 4)
+        for k in range(4)
+    }
+    token_core = {
+        (b, k): remote(
+            tokens if b + k == 0 else block(0, b, k), block(1, b, k), tc_s.at[b, k], tc_r.at[b, k], core
+        )
+        for b in range(4)
+        for k in range(4)
+    }
+    gate_line = [None] + [
+        remote(gates, gate_all.at[k], g_s.at[k], g_r.at[k], on_line[k]) for k in range(1, 4)
+    ]
+    first_line = [None] + [
+        remote(
+            w_in.at[0, :, piece(hid, partner(me_f, k))], first.at[me_f], w1_s.at[k], w1_r.at[k], on_line[k]
+        )
+        for k in range(1, 4)
+    ]
+    second_line = [None] + [
+        remote(
+            w_out.at[0, piece(hid, partner(me_f, k)), :], second.at[k], w2_s.at[k], w2_r.at[k], on_line[k]
+        )
+        for k in range(1, 4)
+    ]
+    own_first = pltpu.make_async_copy(w_in.at[0, :, piece(hid, me_f)], first.at[me_f], loc.at[0])
+    own_second = pltpu.make_async_copy(w_out.at[0, piece(hid, me_f), :], second.at[0], loc.at[1])
+
+    for k in (3, 2, 1):
+        token_line[k].start()
+    for b in range(1, 4):
+        token_plane[b, 0].start()
+    token_core[0, 0].start()
+    for k in (3, 2, 1):
+        first_line[k].start()
+    for k in (3, 2, 1):
+        gate_line[k].start()
+    own_first.start()
+    own_second.start()
+    x[0, 0:rows, :] = tokens[...]
+    gate_all[0, :, :] = gates[...]
+
+    for k in (1, 2, 3):
+        token_line[k].wait_recv()
+        for b in range(1, 4):
+            token_plane[b, k].start()
+        token_core[0, k].start()
+    for k in range(4):
+        for b in range(1, 4):
+            token_plane[b, k].wait_recv()
+            token_core[b, k].start()
+    for k in (1, 2, 3):
+        first_line[k].wait_recv()
+    own_first.wait()
+    for k in (1, 2, 3):
+        second_line[k].start()
+
+    def project(group, carry):
+        hidden = jnp.dot(x[group], first[...].reshape(width, cols), preferred_element_type=jnp.float32)
+        act[group] = gelu(hidden).astype(jnp.bfloat16)
+        return carry
+
+    lax.fori_loop(0, 4, project, 0)
+    for k in range(4):
+        for b in range(4):
+            token_core[b, k].wait_recv()
+    lax.fori_loop(4, 8, project, 0)
+    for copy in list(token_plane.values()) + list(token_core.values()):
+        copy.wait_send()
+    own_second.wait()
+
+    def lane(j):
+        return pl.ds(j * cols, cols)
+
+    sec_copy = [remote(x.at[4:8, :, lane(j)], sec.at[j], sec_s.at[j], sec_r.at[j], core) for j in range(4)]
+    plane_copy = {
+        (j, b): remote(x.at[b, :, lane(j)], plane.at[j, b - 1], pl_s.at[j, b], pl_r.at[j, b], on_plane[b])
+        for j in range(4)
+        for b in range(1, 4)
+    }
+    line_copy = {
+        (j, k): remote(
+            ready.at[j, k], zline.at[j ^ k, k - 1], z_s.at[j, k], z_r.at[j ^ k, k], on_line[k]
+        )
+        for j in range(4)
+        for k in range(1, 4)
+    }
+
+    def expand(j):
+        if j:
+            second_line[j].wait_recv()
+
+        def body(group, carry):
+            value = jnp.dot(act[group], second[j], preferred_element_type=jnp.float32)
+            x[group, :, j * cols:(j + 1) * cols] = value.astype(jnp.bfloat16)
+            return carry
+
+        lax.fori_loop(4, 8, body, 0)
+        sec_copy[j].start()
+        lax.fori_loop(0, 4, body, 0)
+
+    def join_halves(j):
+        sec_copy[j].wait_recv()
+        for b in (3, 1, 2, 0):
+            total = x[b, :, j * cols:(j + 1) * cols].astype(jnp.float32) + sec[j, b].astype(jnp.float32)
+            x[b, :, j * cols:(j + 1) * cols] = total.astype(jnp.bfloat16)
+            if b:
+                plane_copy[j, b].start()
+
+    def join_experts(j):
+        if j == 0:
+            for k in (1, 2, 3):
+                gate_line[k].wait_recv()
+        for b in range(1, 4):
+            plane_copy[j, b].wait_recv()
+        for k in (3, 2, 1, 0):
+            part = slice(k * rows, (k + 1) * rows)
+            total = gate_all[k, :, 0:1] * x[0, part, j * cols:(j + 1) * cols].astype(jnp.float32)
+            for b in range(1, 4):
+                total = total + gate_all[k, :, b:b + 1] * plane[j, b - 1, part, :].astype(jnp.float32)
+            ready[j, k] = total.astype(jnp.bfloat16)
+            if k:
+                line_copy[j, k].start()
+
+    for step in range(6):
+        if step < 4:
+            expand(step)
+        if 0 <= step - 1 < 4:
+            join_halves(step - 1)
+        if 0 <= step - 2 < 4:
+            join_experts(step - 2)
+    for j in range(4):
+        total = ready[j, 0].astype(jnp.float32)
+        for k in range(1, 4):
+            line_copy[j ^ k, k].wait_recv()
+            total = total + zline[j, k - 1].astype(jnp.float32)
+        out[:, pl.ds(pl.multiple_of(partner(me_f, j) * cols, 128), cols)] = total.astype(jnp.bfloat16)
+
+    for copy in token_line[1:] + gate_line[1:] + first_line[1:] + second_line[1:] + sec_copy:
+        copy.wait_send()
+    for copy in list(plane_copy.values()) + list(line_copy.values()):
+        copy.wait_send()
+
+
+def fused(tokens, expert_ids, gate_weights, w_in, w_out):
+    rows, width = tokens.shape
+    lanes = jnp.arange(128, dtype=jnp.int32)
+    expert = jnp.where(lanes < 4, lanes ^ lax.axis_index("egroup"), -1)[None, :]
+    gates = sum(
+        jnp.where(expert_ids[:, i:i + 1] == expert, gate_weights[:, i:i + 1], 0.0) for i in range(2)
+    )
+    cols, hid = width // 4, w_in.shape[2] // 4
+    wide, vmem, dma = jnp.bfloat16, pltpu.VMEM, pltpu.SemaphoreType.DMA
+    return pl.pallas_call(
+        layer_kernel,
+        out_shape=jax.ShapeDtypeStruct((rows, width), wide),
+        in_specs=[
+            pl.BlockSpec(memory_space=pltpu.VMEM),
+            pl.BlockSpec(memory_space=pltpu.VMEM),
+            pl.BlockSpec(memory_space=pl.ANY),
+            pl.BlockSpec(memory_space=pl.ANY),
+        ],
+        out_specs=pl.BlockSpec(memory_space=pltpu.VMEM),
+        scratch_shapes=[
+            vmem((8, 4 * rows, width), wide),
+            vmem((4, cols, hid), wide),
+            vmem((4, hid, cols), wide),
+            vmem((8, 4 * rows, hid), wide),
+            vmem((4, 4, 4 * rows, cols), wide),
+            vmem((4, 3, 4 * rows, cols), wide),
+            vmem((4, 4, rows, cols), wide),
+            vmem((4, 3, rows, cols), wide),
+            vmem((4, rows, 128), jnp.float32),
+        ]
+        + [dma((4,)), dma((4,)), dma((4, 4)), dma((4, 4)), dma((4, 4)), dma((4, 4)), dma((4,)), dma((4,))]
+        + [dma((4,)), dma((4,)), dma((4,)), dma((4,)), dma((4,)), dma((4,))]
+        + [dma((4, 4)), dma((4, 4)), dma((4, 4)), dma((4, 4)), dma((2,))],
+        compiler_params=pltpu.CompilerParams(
+            collective_id=0, has_side_effects=True, vmem_limit_bytes=58 * 2**20
+        ),
+    )(tokens, gates, w_in, w_out)
+
+
+def collective(tokens, expert_ids, gate_weights, w_in, w_out):
     rows, width = tokens.shape
     devices = lax.axis_size("section") * lax.axis_size("egroup") * lax.axis_size("fsdp")
     chunks = 4
@@ -34,6 +272,7 @@
 
 
 def solution(mesh):
+    small = (mesh.shape["section"], mesh.shape["egroup"], mesh.shape["fsdp"]) == (2, 4, 4)
     placed = (
         P(EVERY, None),
         P(EVERY, None),
@@ -42,7 +281,7 @@
         P("egroup", "section", "fsdp"),
     )
     return jax.shard_map(
-        per_device,
+        fused if small else collective,
         mesh=mesh,
         in_specs=placed,
         out_specs=P(EVERY, None),

time: 634 us -> 246 us (0.39)
  waiting for transfers between devices: 278 us -> 0 us
  blocking collectives: 270 us -> 0 us
  Pallas kernels: 0 us -> 241 us
  matrix products: 50.4 us -> 0 us
  between operations: 13.6 us -> 0.01 us
  starting transfers between devices: 8.93 us -> 0 us
  local copies, waits for them, and re-layouts: 10.9 us -> 3.4 us
    reduce_scatter x8 -> x0, waiting for transfers between devices: 277 us -> none  [the longest x4 187 us: per_device(): lax.psum_scatter(result, ('section', 'egroup'), scatter_dimension=0, tile...]
    all_gather x6 -> x0, blocking collectives: 270 us -> none  [the longest x4 105 us: per_device(): part = lax.all_gather(part, 'fsdp', axis=0, tiled=True)]
    pallas_call x0 -> x1, Pallas kernels: none -> 241 us  [fused(): pl.pallas_call(layer_kernel, out_shape=jax.ShapeDtypeStruct((rows, width)...]
    dot_general x4 -> x0, matrix products: 50.4 us -> none  [per_device(): result = jnp.dot(activated, second, preferred_element_type=jnp.float32)]
    all_to_all x2 -> x0, starting transfers between devices: 8.34 us -> none  [the longest x1 4.47 us: per_device(): lax.all_to_all(w_out[0], 'fsdp', split_axis=0, concat_axis=1, tiled=True)]
    all_to_all x2 -> x0, local copies, waits for them, and re-layouts: 6.69 us -> none  [the longest x1 4.29 us: per_device(): lax.all_to_all(w_out[0], 'fsdp', split_axis=0, concat_axis=1, tiled=True)]
  transfers between devices with their start and end apart: 14 -> 0, of which waited for: 8 -> 0; matrix products, arithmetic and copies ran while one was open for 9% -> 0% of each run, Pallas kernels for 0% -> 0%
where the time goes in v2:
time: 246 us; the launch traced here: 245 us
  Pallas kernels  241 us (98%)
  local copies, waits for them, and re-layouts  3.4 us (1%)
    pallas_call x1, Pallas kernels, fused(): pl.pallas_call(layer_kernel, out_shape=jax.ShapeDtypeStruct((rows, width)...  241 us

profile of v2, /device:TPU:0, one launch (start us, length us, event | category | flops | bytes accessed | tf_op | source)
XLA Modules:
  0.0 244.7 jit_solution(14186406551864210805)
XLA Ops:
  0.0 0.8 slice_bitcast_fusion.3
  0.8 0.8 slice_bitcast_fusion.2
  1.5 0.8 select_add_fusion.gates
  2.3 240.5 %shard_map.55 = bf16[128,2048]{1,0:T(8,128)(2,1)} custom-call(bf16[128,2048]{1,0:T(8,128)(2,1)} %tokens.1, f32[128,128]{1,0:T(8,128)} %select_add_fusion.gates, bf16[1,512,2048]{2,1,0:T(8,128)(2,1)} %w_in.1, bf16[1,2048,512]{2,1,0:T(8,128)(2,1)} %w_out.1), custom_call_target="tpu_custom_call" | custom-call | tf_op jit(solution)/shard_map/pallas_call | solution.py:217
  242.8 1.9 copy.7
  (1 shorter events, 0.0 us)

commit v3 on v2

--- a/solution.py
+++ b/solution.py
@@ -26,7 +26,7 @@
 def layer_kernel(
     tokens, gates, w_in, w_out, out,
     x, first, second, act, sec, plane, ready, zline, gate_all,
-    tz_s, tz_r, tp_s, tp_r, tc_s, tc_r, g_s, g_r, w1_s, w1_r, w2_s, w2_r,
+    tz_s, tz_r, tp_s, tp_r, td_s, td_r, tc_s, tc_r, g_s, g_r, w1_s, w1_r, w2_s, w2_r,
     sec_s, sec_r, pl_s, pl_r, z_s, z_r, loc,
 ):
     me_s, me_g, me_f = lax.axis_index("section"), lax.axis_index("egroup"), lax.axis_index("fsdp")
@@ -54,23 +54,35 @@
         return pl.ds(pl.multiple_of(p * (weight // 4), 128), weight // 4)
 
     hid = w_in.shape[2]
-    token_line = [None] + [
-        remote(tokens, block(0, 0, k), tz_s.at[k], tz_r.at[k], on_line[k]) for k in range(1, 4)
-    ]
-    token_plane = {
-        (b, k): remote(
-            tokens if k == 0 else block(0, 0, k), block(0, b, k), tp_s.at[b, k], tp_r.at[b, k], on_plane[b]
-        )
-        for b in range(1, 4)
-        for k in range(4)
-    }
-    token_core = {
-        (b, k): remote(
-            tokens if b + k == 0 else block(0, b, k), block(1, b, k), tc_s.at[b, k], tc_r.at[b, k], core
-        )
-        for b in range(4)
-        for k in range(4)
-    }
+    inner = ((me_f + 1) // 2) % 2
+    is_inner = inner == 1
+    token_next = remote(tokens, block(0, 0, 1), tz_s.at[1], tz_r.at[1], on_line[1])
+    own_across = remote(tokens, block(0, 0, 3), tz_s.at[3], tz_r.at[3], on_line[3])
+    end_across = remote(block(0, 0, 1), block(0, 0, 2), tz_s.at[2], tz_r.at[2], on_line[3])
+    near_out = remote(block(0, 0, 3), block(0, 0, 2), tz_s.at[4], tz_r.at[2], on_line[1])
+    far_out = remote(block(0, 0, 2), block(0, 0, 3), tz_s.at[5], tz_r.at[3], on_line[1])
+
+    def landed(k):
+        return remote(tokens, block(0, 0, k), tz_s.at[0], tz_r.at[k], on_line[1])
+
+    def token_plane(b, k, own=False):
+        return remote(
+            tokens if own else block(0, 0, k), block(0, b, k), tp_s.at[b, k], tp_r.at[b, k], on_plane[b]
+        )
+
+    def half(b, k, part):
+        return x.at[b, pl.ds(k * rows + part * (rows // 2), rows // 2), :]
+
+    def token_corner(part, k):
+        return remote(
+            half(1 + part, k, part), half(3, k, part), td_s.at[part, k], td_r.at[part, k], on_plane[2 - part]
+        )
+
+    def token_core(b, k, own=False):
+        return remote(
+            tokens if own else block(0, b, k), block(1, b, k), tc_s.at[b, k], tc_r.at[b, k], core
+        )
+
     gate_line = [None] + [
         remote(gates, gate_all.at[k], g_s.at[k], g_r.at[k], on_line[k]) for k in range(1, 4)
     ]
@@ -89,11 +101,15 @@
     own_first = pltpu.make_async_copy(w_in.at[0, :, piece(hid, me_f)], first.at[me_f], loc.at[0])
     own_second = pltpu.make_async_copy(w_out.at[0, piece(hid, me_f), :], second.at[0], loc.at[1])
 
-    for k in (3, 2, 1):
-        token_line[k].start()
-    for b in range(1, 4):
-        token_plane[b, 0].start()
-    token_core[0, 0].start()
+    token_next.start()
+
+    @pl.when(is_inner)
+    def _():
+        own_across.start()
+
+    for b in (1, 2):
+        token_plane(b, 0, True).start()
+    token_core(0, 0, True).start()
     for k in (3, 2, 1):
         first_line[k].start()
     for k in (3, 2, 1):
@@ -103,15 +119,36 @@
     x[0, 0:rows, :] = tokens[...]
     gate_all[0, :, :] = gates[...]
 
-    for k in (1, 2, 3):
-        token_line[k].wait_recv()
-        for b in range(1, 4):
-            token_plane[b, k].start()
-        token_core[0, k].start()
-    for k in range(4):
-        for b in range(1, 4):
-            token_plane[b, k].wait_recv()
-            token_core[b, k].start()
+    def spread(k, onward):
+        landed(k).wait_recv()
+
+        @pl.when(is_inner)
+        def _():
+            onward.start()
+
+        for b in (1, 2):
+            token_plane(b, k).start()
+        token_core(0, k).start()
+
+    def corner(k):
+        for part in range(2):
+            token_plane(1 + part, k).wait_recv()
+            token_corner(part, k).start()
+            token_core(1 + part, k).start()
+
+    second_in = 2 + inner
+    third_in = 5 - second_in
+    spread(1, end_across)
+    corner(0)
+    spread(second_in, near_out)
+    corner(1)
+    spread(third_in, far_out)
+    corner(second_in)
+    corner(third_in)
+    for k in (0, 1, second_in, third_in):
+        for part in range(2):
+            token_corner(part, k).wait_recv()
+        token_core(3, k).start()
     for k in (1, 2, 3):
         first_line[k].wait_recv()
     own_first.wait()
@@ -126,10 +163,21 @@
     lax.fori_loop(0, 4, project, 0)
     for k in range(4):
         for b in range(4):
-            token_core[b, k].wait_recv()
+            token_core(b, k).wait_recv()
     lax.fori_loop(4, 8, project, 0)
-    for copy in list(token_plane.values()) + list(token_core.values()):
-        copy.wait_send()
+    for k in range(4):
+        for b in range(4):
+            token_core(b, k).wait_send()
+        for part in range(2):
+            token_plane(1 + part, k).wait_send()
+            token_corner(part, k).wait_send()
+    token_next.wait_send()
+
+    @pl.when(is_inner)
+    def _():
+        for copy in (own_across, end_across, near_out, far_out):
+            copy.wait_send()
+
     own_second.wait()
 
     def lane(j):
@@ -199,7 +247,7 @@
             total = total + zline[j, k - 1].astype(jnp.float32)
         out[:, pl.ds(pl.multiple_of(partner(me_f, j) * cols, 128), cols)] = total.astype(jnp.bfloat16)
 
-    for copy in token_line[1:] + gate_line[1:] + first_line[1:] + second_line[1:] + sec_copy:
+    for copy in gate_line[1:] + first_line[1:] + second_line[1:] + sec_copy:
         copy.wait_send()
     for copy in list(plane_copy.values()) + list(line_copy.values()):
         copy.wait_send()
@@ -235,7 +283,8 @@
             vmem((4, 3, rows, cols), wide),
             vmem((4, rows, 128), jnp.float32),
         ]
-        + [dma((4,)), dma((4,)), dma((4, 4)), dma((4, 4)), dma((4, 4)), dma((4, 4)), dma((4,)), dma((4,))]
+        + [dma((6,)), dma((4,)), dma((4, 4)), dma((4, 4)), dma((2, 4)), dma((2, 4)), dma((4, 4)), dma((4, 4))]
+        + [dma((4,)), dma((4,))]
         + [dma((4,)), dma((4,)), dma((4,)), dma((4,)), dma((4,)), dma((4,))]
         + [dma((4, 4)), dma((4, 4)), dma((4, 4)), dma((4, 4)), dma((2,))],
         compiler_params=pltpu.CompilerParams(

time: 246 us -> 239 us (0.972)
  Pallas kernels: 241 us -> 235 us
    pallas_call x1, Pallas kernels: 241 us -> 235 us  [fused(): pl.pallas_call(layer_kernel, out_shape=jax.ShapeDtypeStruct((rows, width)...]
where the time goes in v3:
time: 239 us
  Pallas kernels  235 us (98%)
  local copies, waits for them, and re-layouts  3.4 us (1%)
    pallas_call x1, Pallas kernels, fused(): pl.pallas_call(layer_kernel, out_shape=jax.ShapeDtypeStruct((rows, width)...  235 us

profile of v3, /device:TPU:0, one launch (start us, length us, event | category | flops | bytes accessed | tf_op | source)
XLA Modules:
  0.0 239.3 jit_solution(15027612922380439842)
XLA Ops:
  0.0 0.8 slice_bitcast_fusion.3
  0.8 0.8 slice_bitcast_fusion.2
  1.5 0.8 select_add_fusion.gates
  2.3 235.1 %shard_map.55 = bf16[128,2048]{1,0:T(8,128)(2,1)} custom-call(bf16[128,2048]{1,0:T(8,128)(2,1)} %tokens.1, f32[128,128]{1,0:T(8,128)} %select_add_fusion.gates, bf16[1,512,2048]{2,1,0:T(8,128)(2,1)} %w_in.1, bf16[1,2048,512]{2,1,0:T(8,128)(2,1)} %w_out.1), custom_call_target="tpu_custom_call" | custom-call | tf_op jit(solution)/shard_map/pallas_call | solution.py:265
  237.4 1.9 copy.7
  (1 shorter events, 0.0 us)

commit v4 on v3

--- a/solution.py
+++ b/solution.py
@@ -25,7 +25,7 @@
 
 def layer_kernel(
     tokens, gates, w_in, w_out, out,
-    x, first, second, act, sec, plane, ready, zline, gate_all,
+    x, first, second, act, sec, plane, ready, zline, gate_all, scale,
     tz_s, tz_r, tp_s, tp_r, td_s, td_r, tc_s, tc_r, g_s, g_r, w1_s, w1_r, w2_s, w2_r,
     sec_s, sec_r, pl_s, pl_r, z_s, z_r, loc,
 ):
@@ -84,8 +84,19 @@
         )
 
     gate_line = [None] + [
-        remote(gates, gate_all.at[k], g_s.at[k], g_r.at[k], on_line[k]) for k in range(1, 4)
+        remote(gates, gate_all.at[0, k], g_s.at[0, k], g_r.at[0, k], on_line[k]) for k in range(1, 4)
     ]
+    gate_plane = {
+        (b, k): remote(
+            gates if k == 0 else gate_all.at[0, k],
+            gate_all.at[b, k],
+            g_s.at[b, k],
+            g_r.at[b, k],
+            on_plane[b],
+        )
+        for b in range(1, 4)
+        for k in range(4)
+    }
     first_line = [None] + [
         remote(
             w_in.at[0, :, piece(hid, partner(me_f, k))], first.at[me_f], w1_s.at[k], w1_r.at[k], on_line[k]
@@ -117,7 +128,9 @@
     own_first.start()
     own_second.start()
     x[0, 0:rows, :] = tokens[...]
-    gate_all[0, :, :] = gates[...]
+    for b in range(1, 4):
+        gate_plane[b, 0].start()
+    gate_all[0, 0] = gates[...]
 
     def spread(k, onward):
         landed(k).wait_recv()
@@ -154,6 +167,10 @@
     own_first.wait()
     for k in (1, 2, 3):
         second_line[k].start()
+    for k in (1, 2, 3):
+        gate_line[k].wait_recv()
+        for b in range(1, 4):
+            gate_plane[b, k].start()
 
     def project(group, carry):
         hidden = jnp.dot(x[group], first[...].reshape(width, cols), preferred_element_type=jnp.float32)
@@ -184,11 +201,21 @@
         return pl.ds(j * cols, cols)
 
     sec_copy = [remote(x.at[4:8, :, lane(j)], sec.at[j], sec_s.at[j], sec_r.at[j], core) for j in range(4)]
-    plane_copy = {
-        (j, b): remote(x.at[b, :, lane(j)], plane.at[j, b - 1], pl_s.at[j, b], pl_r.at[j, b], on_plane[b])
-        for j in range(4)
-        for b in range(1, 4)
-    }
+    def part_rows(part):
+        return pl.ds(part * 2 * rows, 2 * rows)
+
+    plane_copy = {}
+    for j in range(4):
+        for part in range(2):
+            near, far = 1 + part, 2 - part
+            for i, (group, device) in enumerate(((near, near), (3, near), (far, far))):
+                plane_copy[j, part, i] = remote(
+                    x.at[group, part_rows(part), lane(j)],
+                    plane.at[j, i, part_rows(part), :],
+                    pl_s.at[j, part * 3 + i],
+                    pl_r.at[j, part * 3 + i],
+                    on_plane[device],
+                )
     line_copy = {
         (j, k): remote(
             ready.at[j, k], zline.at[j ^ k, k - 1], z_s.at[j, k], z_r.at[j ^ k, k], on_line[k]
@@ -211,35 +238,54 @@
         lax.fori_loop(0, 4, body, 0)
 
     def join_halves(j):
+        if j == 0:
+            for b in range(4):
+                for k in range(4):
+                    if b:
+                        gate_plane[b, k].wait_recv()
+                    scale[b, k * rows:(k + 1) * rows, :] = jnp.transpose(gate_all[b, k])
         sec_copy[j].wait_recv()
         for b in (3, 1, 2, 0):
             total = x[b, :, j * cols:(j + 1) * cols].astype(jnp.float32) + sec[j, b].astype(jnp.float32)
+            total = total * scale[b, :, b:b + 1]
             x[b, :, j * cols:(j + 1) * cols] = total.astype(jnp.bfloat16)
-            if b:
-                plane_copy[j, b].start()
+            if b == 3:
+                plane_copy[j, 0, 1].start()
+                plane_copy[j, 1, 1].start()
+            elif b:
+                plane_copy[j, b - 1, 0].start()
+
+    def pass_on(j):
+        for part in range(2):
+            group, span = 2 - part, slice(part * 2 * rows, (part + 1) * 2 * rows)
+            plane_copy[j, part, 1].wait_recv()
+            total = x[group, span, j * cols:(j + 1) * cols].astype(jnp.float32)
+            total = total + plane[j, 1, span, :].astype(jnp.float32)
+            x[group, span, j * cols:(j + 1) * cols] = total.astype(jnp.bfloat16)
+            plane_copy[j, part, 2].start()
 
     def join_experts(j):
-        if j == 0:
-            for k in (1, 2, 3):
-                gate_line[k].wait_recv()
-        for b in range(1, 4):
-            plane_copy[j, b].wait_recv()
+        for part in range(2):
+            plane_copy[j, part, 0].wait_recv()
+            plane_copy[j, part, 2].wait_recv()
         for k in (3, 2, 1, 0):
-            part = slice(k * rows, (k + 1) * rows)
-            total = gate_all[k, :, 0:1] * x[0, part, j * cols:(j + 1) * cols].astype(jnp.float32)
-            for b in range(1, 4):
-                total = total + gate_all[k, :, b:b + 1] * plane[j, b - 1, part, :].astype(jnp.float32)
+            span = slice(k * rows, (k + 1) * rows)
+            total = x[0, span, j * cols:(j + 1) * cols].astype(jnp.float32)
+            for i in (0, 2):
+                total = total + plane[j, i, span, :].astype(jnp.float32)
             ready[j, k] = total.astype(jnp.bfloat16)
             if k:
                 line_copy[j, k].start()
 
-    for step in range(6):
-        if step < 4:
-            expand(step)
+    for step in range(7):
         if 0 <= step - 1 < 4:
             join_halves(step - 1)
         if 0 <= step - 2 < 4:
-            join_experts(step - 2)
+            pass_on(step - 2)
+        if 0 <= step - 3 < 4:
+            join_experts(step - 3)
+        if step < 4:
+            expand(step)
     for j in range(4):
         total = ready[j, 0].astype(jnp.float32)
         for k in range(1, 4):
@@ -249,17 +295,15 @@
 
     for copy in gate_line[1:] + first_line[1:] + second_line[1:] + sec_copy:
         copy.wait_send()
-    for copy in list(plane_copy.values()) + list(line_copy.values()):
+    for copy in list(gate_plane.values()) + list(plane_copy.values()) + list(line_copy.values()):
         copy.wait_send()
 
 
 def fused(tokens, expert_ids, gate_weights, w_in, w_out):
     rows, width = tokens.shape
-    lanes = jnp.arange(128, dtype=jnp.int32)
-    expert = jnp.where(lanes < 4, lanes ^ lax.axis_index("egroup"), -1)[None, :]
-    gates = sum(
-        jnp.where(expert_ids[:, i:i + 1] == expert, gate_weights[:, i:i + 1], 0.0) for i in range(2)
-    )
+    steps = jnp.arange(8, dtype=jnp.int32)
+    expert = jnp.where(steps < 4, steps ^ lax.axis_index("egroup"), -1)[:, None]
+    gates = sum(jnp.where(expert_ids[:, i][None, :] == expert, gate_weights[:, i][None, :], 0.0) for i in range(2))
     cols, hid = width // 4, w_in.shape[2] // 4
     wide, vmem, dma = jnp.bfloat16, pltpu.VMEM, pltpu.SemaphoreType.DMA
     return pl.pallas_call(
@@ -281,12 +325,13 @@
             vmem((4, 3, 4 * rows, cols), wide),
             vmem((4, 4, rows, cols), wide),
             vmem((4, 3, rows, cols), wide),
-            vmem((4, rows, 128), jnp.float32),
+            vmem((4, 4, 8, rows), jnp.float32),
+            vmem((4, 4 * rows, 8), jnp.float32),
         ]
         + [dma((6,)), dma((4,)), dma((4, 4)), dma((4, 4)), dma((2, 4)), dma((2, 4)), dma((4, 4)), dma((4, 4))]
-        + [dma((4,)), dma((4,))]
+        + [dma((4, 4)), dma((4, 4))]
         + [dma((4,)), dma((4,)), dma((4,)), dma((4,)), dma((4,)), dma((4,))]
-        + [dma((4, 4)), dma((4, 4)), dma((4, 4)), dma((4, 4)), dma((2,))],
+        + [dma((4, 6)), dma((4, 6)), dma((4, 4)), dma((4, 4)), dma((2,))],
         compiler_params=pltpu.CompilerParams(
             collective_id=0, has_side_effects=True, vmem_limit_bytes=58 * 2**20
         ),

time: 239 us -> 215 us (0.90)
  Pallas kernels: 235 us -> 211 us
    pallas_call x1, Pallas kernels: 235 us -> 211 us  [fused(): pl.pallas_call(layer_kernel, out_shape=jax.ShapeDtypeStruct((rows, width)...]
where the time goes in v4:
time: 215 us
  Pallas kernels  211 us (98%)
  local copies, waits for them, and re-layouts  3.4 us (2%)
    pallas_call x1, Pallas kernels, fused(): pl.pallas_call(layer_kernel, out_shape=jax.ShapeDtypeStruct((rows, width)...  211 us

profile of v4, /device:TPU:0, one launch (start us, length us, event | category | flops | bytes accessed | tf_op | source)
XLA Modules:
  0.0 214.8 jit_solution(9163496510432085525)
XLA Ops:
  0.0 0.8 slice_bitcast_fusion.3
  0.8 0.8 slice_bitcast_fusion.2
  1.5 0.7 select_add_fusion.gates
  2.2 210.8 %shard_map.55 = bf16[128,2048]{1,0:T(8,128)(2,1)} custom-call(bf16[128,2048]{1,0:T(8,128)(2,1)} %tokens.1, f32[8,128]{1,0:T(8,128)} %select_add_fusion.gates, bf16[1,512,2048]{2,1,0:T(8,128)(2,1)} %w_in.1, bf16[1,2048,512]{2,1,0:T(8,128)(2,1)} %w_out.1), custom_call_target="tpu_custom_call" | custom-call | tf_op jit(solution)/shard_map/pallas_call | solution.py:309
  213.0 1.9 copy.7
  (1 shorter events, 0.0 us)

commit v5 on v4

--- a/solution.py
+++ b/solution.py
@@ -122,8 +122,6 @@
         token_plane(b, 0, True).start()
     token_core(0, 0, True).start()
     for k in (3, 2, 1):
-        first_line[k].start()
-    for k in (3, 2, 1):
         gate_line[k].start()
     own_first.start()
     own_second.start()
@@ -156,6 +154,8 @@
     spread(second_in, near_out)
     corner(1)
     spread(third_in, far_out)
+    for k in (3, 2, 1):
+        first_line[k].start()
     corner(second_in)
     corner(third_in)
     for k in (0, 1, second_in, third_in):

time: 215 us -> 189 us (0.88)
  Pallas kernels: 211 us -> 185 us
    pallas_call x1, Pallas kernels: 211 us -> 185 us  [fused(): pl.pallas_call(layer_kernel, out_shape=jax.ShapeDtypeStruct((rows, width)...]
where the time goes in v5:
time: 189 us
  Pallas kernels  185 us (98%)
  local copies, waits for them, and re-layouts  3.4 us (2%)
    pallas_call x1, Pallas kernels, fused(): pl.pallas_call(layer_kernel, out_shape=jax.ShapeDtypeStruct((rows, width)...  185 us

profile of v5, /device:TPU:0, one launch (start us, length us, event | category | flops | bytes accessed | tf_op | source)
XLA Modules:
  0.0 188.9 jit_solution(6176110601286430047)
XLA Ops:
  0.0 0.8 slice_bitcast_fusion.3
  0.8 0.8 slice_bitcast_fusion.2
  1.5 0.7 select_add_fusion.gates
  2.2 184.9 %shard_map.55 = bf16[128,2048]{1,0:T(8,128)(2,1)} custom-call(bf16[128,2048]{1,0:T(8,128)(2,1)} %tokens.1, f32[8,128]{1,0:T(8,128)} %select_add_fusion.gates, bf16[1,512,2048]{2,1,0:T(8,128)(2,1)} %w_in.1, bf16[1,2048,512]{2,1,0:T(8,128)(2,1)} %w_out.1), custom_call_target="tpu_custom_call" | custom-call | tf_op jit(solution)/shard_map/pallas_call | solution.py:309
  187.1 1.9 copy.7
  (1 shorter events, 0.0 us)
